TPU v7x, 32 devices: a whole 2x2x4 slice. The times are simulated.
32 devices in a mesh: expert: 4 (over x, core), tensor: 4 (over z), kv: 2 (over y).
Axes of the slice: x: 2, y: 2, z: 4, core: 2. Of those that a mesh axis runs over, the one named last changes fastest.
Arguments:
- residual_stream: bfloat16 [1024, 4096], P('expert', ('tensor', 'kv')), may hold values from -13 to 13
- grad_output: bfloat16 [1024, 4096], P('expert', ('tensor', 'kv')), may hold values from -6 to 6
- norm_gain: bfloat16 [4096], P(('tensor', 'kv')), may hold values from 0.5 to 1.5
- expert_ids: int32 [1024, 2], P('expert'), may hold values from 0 to 3, all different within a row; in each aligned block of 256 rows (0 to 255, 256 to 511, ...) at most 160 rows name the same one
- gate_probs: float32 [1024, 2], P('expert'), may hold values from 0.1 to 0.9
- w_gate: bfloat16 [4, 14336, 4096], P('expert', ('tensor', 'kv')), may hold values from -0.125 to 0.125
- w_up: bfloat16 [4, 14336, 4096], P('expert', ('tensor', 'kv')), may hold values from -0.125 to 0.125
- w_down: bfloat16 [4, 14336, 4096], P('expert', ('tensor', 'kv')), may hold values from -0.046875 to 0.046875
Outputs:
- input_grad: bfloat16 [1024, 4096], P('expert', ('tensor', 'kv'))
Inputs may be any that keep to these rules, and one draw needn't show every extreme that they name: `expert_ids`: each row names two different experts. In each aligned block of 256 rows (the rows of one index of the expert axis) no expert is named by more than 160 rows, a bound that some block reaches.
All inputs are finite; a program needn't handle non-finite values.
Results may differ from a plain program's by a relative error of at most 0.018.
Values may be sent and summed in bfloat16 or wider, within the bound.
A program may use at most 128 MiB of HBM per device.

v0:
```python
import functools

import jax
import jax.numpy as jnp
from jax import lax
from jax.experimental import pallas as pl
from jax.experimental.pallas import tpu as pltpu
from jax.sharding import PartitionSpec as P

D = 4096
CAP = 160


epsilon = 1e-05
contract_width = (((1,), (1,)), ((), ()))
contract_hidden = (((0,), (1,)), ((), ()))
contract_slots = (((0,), (0,)), ((), ()))


def slot_matrix(ids_block, experts):
    flattened = ids_block.reshape(-1)
    onehot = (flattened[:, None] == jnp.arange(experts, dtype=jnp.int32)[None, :]).astype(jnp.int32)
    before = jnp.cumsum(onehot, axis=0) - onehot
    position = jnp.sum(before * onehot, axis=1)
    slot_index = flattened * CAP + position
    table = jnp.arange(experts * CAP, dtype=jnp.int32)
    return (slot_index[None, :] == table[:, None]).astype(jnp.bfloat16)


def shards(residual_stream, grad_output, norm_gain, expert_ids, gate_probs, w_gate, w_up, w_down):
    experts = lax.axis_size("expert")
    local_width = residual_stream.shape[1]
    tokens_here = residual_stream.shape[0]
    stream = residual_stream.astype(jnp.float32)
    squares = lax.psum(jnp.sum(stream * stream, axis=1), ("tensor", "kv"))
    inverse_rms = lax.rsqrt(squares / D + epsilon)[:, None]
    gains = norm_gain.astype(jnp.float32)
    normed = (stream * inverse_rms * gains).astype(jnp.bfloat16)
    table = slot_matrix(expert_ids, experts)
    repeated_x = jnp.repeat(normed, 2, axis=0)
    scaled = (
        jnp.repeat(grad_output.astype(jnp.float32), 2, axis=0) * gate_probs.reshape(-1, 1)
    ).astype(jnp.bfloat16)
    routed_x = jnp.dot(table, repeated_x, preferred_element_type=jnp.float32).astype(jnp.bfloat16)
    routed_grad = jnp.dot(table, scaled, preferred_element_type=jnp.float32).astype(jnp.bfloat16)
    routed_x = routed_x.reshape(experts, CAP, local_width)
    routed_grad = routed_grad.reshape(experts, CAP, local_width)
    gate_weight, up_weight, down_weight = (w_gate[0], w_up[0], w_down[0])
    pieces_x = lax.all_to_all(routed_x, "expert", split_axis=0, concat_axis=0, tiled=True)
    pieces_dy = lax.all_to_all(routed_grad, "expert", split_axis=0, concat_axis=0, tiled=True)
    full_x = lax.all_gather(pieces_x, ("tensor", "kv"), axis=2, tiled=True)
    full_dy = lax.all_gather(pieces_dy, ("tensor", "kv"), axis=2, tiled=True)
    leading = full_x.shape[0]
    items = full_x.shape[1]
    matrix_x = full_x.reshape(leading * items, D)
    matrix_dy = full_dy.reshape(leading * items, D)
    gate_value = lax.dot_general(
        matrix_x, gate_weight, contract_width, preferred_element_type=jnp.float32
    )
    up_value = lax.dot_general(
        matrix_x, up_weight, contract_width, preferred_element_type=jnp.float32
    )
    act_grad = lax.dot_general(
        matrix_dy, down_weight, contract_width, preferred_element_type=jnp.float32
    )
    sigmoid_gate = jax.nn.sigmoid(gate_value)
    activated = gate_value * sigmoid_gate
    gate_grad = (
        act_grad * up_value * sigmoid_gate * (1.0 + gate_value * (1.0 - sigmoid_gate))
    ).astype(jnp.bfloat16)
    up_grad = (act_grad * activated).astype(jnp.bfloat16)
    total = lax.dot_general(
        gate_weight, gate_grad, contract_hidden, preferred_element_type=jnp.float32
    )
    summed = lax.psum_scatter(
        total
        + lax.dot_general(up_weight, up_grad, contract_hidden, preferred_element_type=jnp.float32),
        ("tensor", "kv"),
        scatter_dimension=0,
        tiled=True,
    )
    returned = summed.T.astype(jnp.bfloat16).reshape(leading, items, local_width)
    combined = lax.all_to_all(returned, "expert", split_axis=0, concat_axis=0, tiled=True)
    gathered = lax.dot_general(
        table,
        combined.reshape(experts * CAP, local_width),
        contract_slots,
        preferred_element_type=jnp.float32,
    )
    token_grad = gathered.reshape(tokens_here, 2, local_width).sum(axis=1)
    scaled_grad = token_grad * gains
    projection = lax.psum(jnp.sum(scaled_grad * stream, axis=1), ("tensor", "kv"))[:, None]
    result = inverse_rms * scaled_grad - stream * inverse_rms**3 * projection / D
    return result.astype(jnp.bfloat16)


MESH = pl.DeviceIdType.MESH
TILE = 256


def fused_kernel(
    T, x_ref, dy_ref, gain_ref, meta_ref, wg_ref, wu_ref, wd_ref, out_ref,
    tok, acc, wbuf, hid, routed, crecv, xrecv, yrecv, zrecv, gains, metas, sel, prob,
    ssq, own_sq, psend, precv,
    ag_send, ag_recv, line_send, line_recv, rs_send, rs_recv, small_send, small_recv, wsem, lsem,
):
    e = lax.axis_index("expert")
    z = lax.axis_index("tensor")
    y = lax.axis_index("kv")
    core = e + 1 - 2 * lax.rem(e, 2)
    across = lax.rem(e + 2, 4)
    width = x_ref.shape[1]
    hidden = wg_ref.shape[0]
    tiles = hidden // TILE
    blocks = 2 * T
    inputs = (x_ref, dy_ref)

    def z_of(d):
        return lax.rem(z + T - d, T)

    nearer_low = z < T - 1 - z
    reach = jnp.where(nearer_low, z, T - 1 - z)

    def visit(d):
        if d == 0:
            return z
        near = z + (d + 1) // 2 if d % 2 else z - d // 2
        far = jnp.where(nearer_low, d, T - 1 - d)
        return jnp.where(d <= 2 * reach, near, far)

    def y_of(s):
        return y if s == 0 else 1 - y

    def fb_of(d, s):
        return z_of(d) * 2 + y_of(s)

    def seen(d, s):
        return visit(d) * 2 + y_of(s)

    def b_of(u, c):
        base = core if c else e
        return lax.rem(base + 2 * u, 4)

    def slot(a, d, s, u, c):
        return tok.at[a, seen(d, s), b_of(u, c)]

    def number(a, d, s, u, c):
        return (((a * T + d) * 2 + s) * 2 + u) * 2 + c

    def plan(a, d, s, u, c):
        if c:
            return (d, s, u, 0), (core, z, y)
        if a == 0:
            if u:
                return (d, s, 0, 0), (across, z, y)
            if s:
                return (d, 0, 0, 0), (e, z, 1 - y)
        else:
            if s:
                return (d, 0, u, 0), (e, z, 1 - y)
            if u:
                return (d, 0, 0, 0), (across, z, y)
        raise ValueError(d)

    def gather_copy(a, d, s, u, c):
        source, target = plan(a, d, s, u, c)
        n = number(a, d, s, u, c)
        fb, b = seen(*source[:2]), b_of(*source[2:])
        src = inputs[a] if source == (0, 0, 0, 0) else tok.at[a, fb, b]
        return pltpu.make_async_remote_copy(
            src_ref=src, dst_ref=tok.at[a, fb, b],
            send_sem=ag_send.at[n], recv_sem=ag_recv.at[n],
            device_id=target, device_id_type=MESH,
        )

    def gather_wait(a, d, s, u, c):
        n = number(a, d, s, u, c)
        here = slot(a, d, s, u, c)
        pltpu.make_async_remote_copy(
            src_ref=here, dst_ref=here, send_sem=ag_send.at[n], recv_sem=ag_recv.at[n],
            device_id=plan(a, d, s, u, c)[1], device_id_type=MESH,
        ).wait_recv()

    steps = [(d, s) for d in range(T) for s in (0, 1)]
    back = [(d, s) for d in list(range(1, T)) + [0] for s in (1, 0)]

    def weight_copies(step):
        if step < blocks:
            fb, refs = seen(*steps[step]), (wg_ref, wu_ref, wd_ref)
        else:
            fb, refs = fb_of(*back[step - blocks]), (wg_ref, wu_ref)
        columns = pl.ds(pl.multiple_of(fb * width, width), width)
        return [
            pltpu.make_async_copy(ref.at[:, columns], wbuf.at[step % 2, k], wsem.at[step % 2, k])
            for k, ref in enumerate(refs)
        ]

    for copy in weight_copies(0):
        copy.start()
    local = [
        pltpu.make_async_copy(x_ref, tok.at[0, fb_of(0, 0), e], lsem.at[0]),
        pltpu.make_async_copy(dy_ref, tok.at[1, fb_of(0, 0), e], lsem.at[1]),
        pltpu.make_async_copy(gain_ref, gains.at[fb_of(0, 0)], lsem.at[2]),
        pltpu.make_async_copy(meta_ref, metas.at[e], lsem.at[3]),
    ]
    for copy in local:
        copy.start()

    peers = [(e, lax.rem(z + d, T), y_of(s)) for d in range(T) for s in (0, 1) if d or s]
    sources = [fb_of(d, s) for d in range(T) for s in (0, 1) if d or s]
    others = [(lax.rem(e + k, 4), z, y) for k in (1, 2, 3)]
    barrier = pltpu.get_barrier_semaphore()
    for peer in peers + others:
        pl.semaphore_signal(barrier, inc=1, device_id=peer, device_id_type=MESH)
    pl.semaphore_wait(barrier, len(peers) + len(others))

    def remote(src, dst, send, recv, peer):
        return pltpu.make_async_remote_copy(
            src_ref=src, dst_ref=dst, send_sem=send, recv_sem=recv,
            device_id=peer, device_id_type=MESH,
        )

    small = []
    for k, peer in enumerate(others):
        copy = remote(meta_ref, metas.at[e], small_send.at[k], small_recv.at[k], peer)
        copy.start()
        there = metas.at[lax.rem(e + 3 - k, 4)]
        small.append((copy, remote(there, there, small_send.at[k], small_recv.at[k], peer)))

    def own_line(a, way):
        fb = fb_of(0, 0)
        return remote(
            inputs[a], tok.at[a, fb, e], line_send.at[a, way], line_recv.at[a, z],
            (e, z + 2 * way - 1, y),
        )

    def pass_on(a, d):
        v = visit(d)
        here = tok.at[a, seen(d, 0), e]
        return remote(
            here, here, line_send.at[a, 1 + d], line_recv.at[a, v],
            (e, jnp.where(v < z, z + 1, z - 1), y),
        )

    def passes(d):
        v = visit(d)
        return jnp.where(v < z, z < T - 1, z > 0)

    for a in (0, 1):
        for way in (0, 1):
            @pl.when(z < T - 1 if way else z > 0)
            def _():
                own_line(a, way).start()

    def arrive(a, d):
        pass_on(a, d).wait_recv()

        @pl.when(passes(d))
        def _():
            pass_on(a, d).start()

    for k, peer in enumerate(peers):
        n = 3 + k
        copy = remote(gain_ref, gains.at[fb_of(0, 0)], small_send.at[n], small_recv.at[n], peer)
        copy.start()
        there = gains.at[sources[k]]
        small.append((copy, remote(there, there, small_send.at[n], small_recv.at[n], peer)))

    def level1(d):
        if d:
            arrive(0, d)
        gather_copy(0, d, 1, 0, 0).start()
        if d:
            arrive(1, d)
        gather_copy(1, d, 0, 1, 0).start()
        gather_copy(0, d, 0, 1, 0).start()
        gather_copy(1, d, 1, 0, 0).start()
        gather_copy(0, d, 0, 0, 1).start()
        gather_copy(1, d, 0, 0, 1).start()

    def level2(d):
        gather_wait(0, d, 1, 0, 0)
        gather_copy(0, d, 1, 1, 0).start()
        gather_copy(0, d, 1, 0, 1).start()
        gather_wait(1, d, 0, 1, 0)
        gather_copy(1, d, 1, 1, 0).start()
        gather_copy(1, d, 0, 1, 1).start()

    def level3(d):
        gather_wait(0, d, 0, 1, 0)
        gather_copy(0, d, 0, 1, 1).start()
        gather_wait(1, d, 1, 0, 0)
        gather_copy(1, d, 1, 0, 1).start()
        gather_wait(0, d, 1, 1, 0)
        gather_copy(0, d, 1, 1, 1).start()
        gather_wait(1, d, 1, 1, 0)
        gather_copy(1, d, 1, 1, 1).start()

    def multiply(step):
        d, s = steps[step]
        for copy in weight_copies(step + 1):
            copy.start()
        for a in (0, 1):
            for u in (0, 1):
                gather_wait(a, d, s, u, 1)
        fb = seen(d, s)
        gain_row = gains[fb, 0:1, :]
        mine = tok[0, fb, e].astype(jnp.float32)
        own_sq[...] += jnp.sum(mine * mine, axis=1, keepdims=True)
        for b in range(4):
            rows = pl.ds(b * CAP, CAP)
            picked = jnp.dot(sel[b], tok[0, fb, b], preferred_element_type=jnp.float32)
            ssq[rows, :] += jnp.sum(picked * picked, axis=1, keepdims=True)
            routed[0, rows, :] = (picked * gain_row).astype(jnp.bfloat16)
            picked = jnp.dot(sel[b], tok[1, fb, b], preferred_element_type=jnp.float32)
            routed[1, rows, :] = (picked * prob[rows, :]).astype(jnp.bfloat16)
        for copy in weight_copies(step):
            copy.wait()

        def tile(n, carry):
            rows = pl.ds(pl.multiple_of(n * TILE, TILE), TILE)
            for k in range(3):
                term = lax.dot_general(
                    routed[k // 2], wbuf[step % 2, k, rows, :], contract_width,
                    preferred_element_type=jnp.float32,
                )
                if step == 0:
                    acc[k, n] = term
                else:
                    acc[k, n] += term
            return carry

        lax.fori_loop(0, tiles, tile, 0)

    level1(0)
    level2(0)
    for copy in local:
        copy.wait()
    for copy, arrival in small[:3]:
        arrival.wait_recv()
    own_sq[...] = jnp.zeros_like(own_sq)
    ssq[...] = jnp.zeros_like(ssq)
    for b in range(4):
        slots = metas[b, pl.ds(e, 1), :]
        probs = metas[b, pl.ds(4 + e, 1), :]
        index = lax.broadcasted_iota(jnp.int32, (CAP, slots.shape[1]), 0).astype(jnp.float32)
        chosen = jnp.where(index == slots, 1.0, 0.0)
        sel[b] = chosen.astype(jnp.bfloat16)
        prob[pl.ds(b * CAP, CAP), :] = jnp.sum(chosen * probs, axis=1, keepdims=True)
    for copy, arrival in small[3:]:
        arrival.wait_recv()
    level1(1)
    level3(0)
    multiply(0)
    level2(1)
    level1(2)
    for d in range(3, T):
        level1(d)
    multiply(1)
    level3(1)
    for d in range(2, T):
        multiply(2 * d - 2)
        level2(d)
        multiply(2 * d - 1)
        level3(d)
    multiply(blocks - 2)
    multiply(blocks - 1)
    for a in (0, 1):
        for n in range(1, blocks * 4):
            c, u, s, d = n % 2, n // 2 % 2, n // 4 % 2, n // 8
            if s or u or c:
                gather_copy(a, d, s, u, c).wait_send()
        for way in (0, 1):
            @pl.when(z < T - 1 if way else z > 0)
            def _():
                own_line(a, way).wait_send()
        for d in range(1, T):
            @pl.when(passes(d))
            def _():
                pass_on(a, d).wait_send()
    for copy, arrival in small:
        copy.wait_send()

    inverse = lax.rsqrt(ssq[...] / D + epsilon)

    def activate(n, carry):
        columns = pl.ds(pl.multiple_of(n * TILE, TILE), TILE)
        gate_value = acc[0, n] * inverse
        up_value = acc[1, n] * inverse
        act_grad = acc[2, n]
        sigmoid_gate = jax.nn.sigmoid(gate_value)
        hid[0, :, columns] = (
            act_grad * up_value * sigmoid_gate * (1.0 + gate_value * (1.0 - sigmoid_gate))
        ).astype(jnp.bfloat16)
        hid[1, :, columns] = (act_grad * gate_value * sigmoid_gate).astype(jnp.bfloat16)
        return carry

    lax.fori_loop(0, tiles, activate, 0)

    def core_copy(i, u):
        return remote(
            tok.at[0, i, lax.rem(core + 2 * u, 4)], crecv.at[i, u],
            rs_send.at[i, u], rs_recv.at[i, u], (core, z, y),
        )

    def across_copy(i):
        return remote(tok.at[1, i, 0], xrecv.at[i], rs_send.at[i, 2], rs_recv.at[i, 2], (across, z, y))

    def pair_copy(i):
        d = back[i][0]
        return remote(tok.at[1, i, 1], yrecv.at[d], rs_send.at[i, 3], rs_recv.at[i, 3], (e, z, 1 - y))

    def line_copy(i):
        d = back[i][0]
        return remote(
            tok.at[1, i, 2], zrecv.at[d - 1], rs_send.at[i, 4], rs_recv.at[i, 4], (e, z_of(d), y)
        )

    def produce(i):
        step = blocks + i
        if i + 1 < blocks:
            for copy in weight_copies(step + 1):
                copy.start()
        for copy in weight_copies(step):
            copy.wait()

        def tile(n, carry):
            columns = pl.ds(pl.multiple_of(n * TILE, TILE), TILE)
            total = jnp.dot(
                hid[0], wbuf[step % 2, 0, :, columns], preferred_element_type=jnp.float32
            ) + jnp.dot(hid[1], wbuf[step % 2, 1, :, columns], preferred_element_type=jnp.float32)
            rounded = total.astype(jnp.bfloat16)
            for b in range(4):
                tok[0, i, b, :, columns] = lax.dot_general(
                    sel[b], rounded[b * CAP : (b + 1) * CAP], contract_slots,
                    preferred_element_type=jnp.float32,
                ).astype(jnp.bfloat16)
            return carry

        lax.fori_loop(0, width // TILE, tile, 0)
        core_copy(i, 1).start()
        core_copy(i, 0).start()

    def combine_cores(i):
        core_copy(i, 1).wait_recv()
        tok[1, i, 0] = (
            tok[0, i, across].astype(jnp.float32) + crecv[i, 1].astype(jnp.float32)
        ).astype(jnp.bfloat16)
        across_copy(i).start()

    def combine_across(i):
        d, s = back[i]
        core_copy(i, 0).wait_recv()
        across_copy(i).wait_recv()
        value = (
            tok[0, i, e].astype(jnp.float32)
            + crecv[i, 0].astype(jnp.float32)
            + xrecv[i].astype(jnp.float32)
        )
        if s:
            tok[1, i, 1] = value.astype(jnp.bfloat16)
            pair_copy(i).start()
            return None
        pair_copy(i - 1).wait_recv()
        value = value + yrecv[d].astype(jnp.float32)
        if d:
            tok[1, i, 2] = value.astype(jnp.bfloat16)
            line_copy(i).start()
            return None
        return value

    value = None
    for i in range(blocks + 2):
        if i < blocks:
            produce(i)
        if 1 <= i <= blocks:
            combine_cores(i - 1)
        if i >= 2:
            value = combine_across(i - 2)
    for i in range(blocks):
        if back[i][1] == 0 and back[i][0]:
            line_copy(i).wait_recv()
            value = value + zrecv[back[i][0] - 1].astype(jnp.float32)

    gain_row = gains[fb_of(0, 0), 0:1, :]
    stream = x_ref[...].astype(jnp.float32)
    scaled = value * gain_row
    share = jnp.sum(scaled * stream, axis=1, keepdims=True)
    tokens = stream.shape[0]
    psend[...] = jnp.broadcast_to(share, (tokens, 128)).T[0:8, :]
    final = []
    for k, peer in enumerate(peers):
        n = 3 + len(peers) + k
        copy = remote(psend, precv.at[k], small_send.at[n], small_recv.at[n], peer)
        copy.start()
        final.append(copy)
    inverse = lax.rsqrt(own_sq[...] / D + epsilon)
    row = psend[...]
    for k, copy in enumerate(final):
        copy.wait_recv()
        row = row + precv[k]
    projection = jnp.broadcast_to(row[0:1, :], (128, tokens)).T[:, 0:1]
    out_ref[...] = (
        inverse * scaled - stream * (inverse * inverse * inverse * projection / D)
    ).astype(out_ref.dtype)
    for copy in final:
        copy.wait_send()
    for i in range(blocks):
        core_copy(i, 0).wait_send()
        core_copy(i, 1).wait_send()
        across_copy(i).wait_send()
        if back[i][1]:
            pair_copy(i).wait_send()
        elif back[i][0]:
            line_copy(i).wait_send()


def fused_shards(residual_stream, grad_output, norm_gain, expert_ids, gate_probs, w_gate, w_up, w_down):
    experts = lax.axis_size("expert")
    T = lax.axis_size("tensor")
    blocks = 2 * T
    tokens, width = residual_stream.shape
    hidden = w_gate.shape[1]
    numbers = jnp.arange(experts, dtype=jnp.int32)
    onehot = (expert_ids[:, :, None] == numbers[None, None, :]).astype(jnp.int32)
    named = onehot.sum(axis=1)
    before = jnp.cumsum(named, axis=0) - named
    slots = jnp.where(named > 0, before, -1).astype(jnp.float32)
    probs = jnp.sum(gate_probs[:, :, None] * onehot.astype(jnp.float32), axis=1)
    meta = jnp.concatenate([slots.T, probs.T], axis=0)
    gain = jnp.broadcast_to(norm_gain.astype(jnp.float32)[None, :], (8, width))
    bf16, f32 = jnp.bfloat16, jnp.float32
    rows = experts * CAP
    vmem = pl.BlockSpec(memory_space=pltpu.VMEM)
    hbm = pl.BlockSpec(memory_space=pl.ANY)
    dma = pltpu.SemaphoreType.DMA
    unit = (tokens, width)
    smalls = 3 + 2 * (blocks - 1)
    return pl.pallas_call(
        functools.partial(fused_kernel, T),
        out_shape=jax.ShapeDtypeStruct(unit, bf16),
        in_specs=[vmem] * 4 + [hbm] * 3,
        out_specs=vmem,
        scratch_shapes=[
            pltpu.VMEM((2, blocks, experts) + unit, bf16),
            pltpu.VMEM((3, hidden // TILE, rows, TILE), f32),
            pltpu.VMEM((2, 3, hidden, width), bf16),
            pltpu.VMEM((2, rows, hidden), bf16),
            pltpu.VMEM((2, rows, width), bf16),
            pltpu.VMEM((blocks, 2) + unit, bf16),
            pltpu.VMEM((blocks,) + unit, bf16),
            pltpu.VMEM((T,) + unit, bf16),
            pltpu.VMEM((T - 1,) + unit, bf16),
            pltpu.VMEM((blocks, 8, width), f32),
            pltpu.VMEM((experts, 8, tokens), f32),
            pltpu.VMEM((experts, CAP, tokens), bf16),
            pltpu.VMEM((rows, 1), f32),
            pltpu.VMEM((rows, 1), f32),
            pltpu.VMEM((tokens, 1), f32),
            pltpu.VMEM((8, tokens), f32),
            pltpu.VMEM((blocks - 1, 8, tokens), f32),
            dma((16 * T,)),
            dma((16 * T,)),
            dma((2, T + 1)),
            dma((2, T)),
            dma((blocks, 5)),
            dma((blocks, 5)),
            dma((smalls,)),
            dma((smalls,)),
            dma((2, 3)),
            dma((4,)),
        ],
        compiler_params=pltpu.CompilerParams(
            collective_id=0, has_side_effects=True, vmem_limit_bytes=66000000
        ),
        name="fused",
    )(residual_stream, grad_output, gain, meta, w_gate[0], w_up[0], w_down[0])


def solution(mesh):
    placed = (
        P("expert", ("tensor", "kv")),
        P("expert", ("tensor", "kv")),
        P(("tensor", "kv")),
        P("expert", None),
        P("expert", None),
        P("expert", ("tensor", "kv"), None),
        P("expert", ("tensor", "kv"), None),
        P("expert", ("tensor", "kv"), None),
    )
    sizes = dict(mesh.shape)
    width = D // (sizes["tensor"] * sizes["kv"])
    body = fused_shards if sizes["expert"] == 4 and sizes["kv"] == 2 and width % 256 == 0 else shards
    return jax.shard_map(
        body, mesh=mesh, in_specs=placed, out_specs=P("expert", ("tensor", "kv")), check_vma=False
    )
```

profile of v0, /device:TPU:0, one launch (start us, length us, event | category | flops | bytes accessed | tf_op | source)
XLA Modules:
  0.0 172.3 jit_solution(2180676208821561695)
XLA Ops:
  0.0 0.7 convert_reduce_fusion
  0.7 1.2 reduce-window.6
  1.9 0.1 slice.8
  2.0 0.1 copy.13
  2.1 0.1 copy.14
  2.2 0.1 add_bitcast_fusion
  2.3 0.7 fusion.1
  3.0 0.6 pad_maximum_fusion.meta_ref
  3.6 1.3 broadcast_in_dim.6.gain_ref
  4.9 165.7 %fused.1 = bf16[256,512]{1,0:T(8,128)(2,1)} custom-call(bf16[256,512]{1,0:T(8,128)(2,1)} %x_ref.1, bf16[256,512]{1,0:T(8,128)(2,1)} %dy_ref.1, f32[8,512]{1,0:T(8,128)} %broadcast_in_dim.6.gain_ref, f32[8,256]{1,0:T(8,128)} %pad_maximum_fusion.meta_ref, bf16[1792,4096]{1,0:T(8,128)(2,1)} %bitcast.15, bf16[1792,4096]{1,0:T(8,128)(2,1)} %bitcast.16, ...), custom_call_target="tpu_custom_call" | custom-call | tf_op jit(solution)/shard_map/fused/pallas_call | solution.py:539
  170.7 1.7 copy.18
  (4 shorter events, 0.1 us)
where the time goes:
time: 173 us; the launch traced here: 172 us
  Pallas kernels  166 us (96%)
  other arithmetic  3.34 us (2%)
  local copies, waits for them, and re-layouts  3.25 us (2%)
    pallas_call x1, Pallas kernels, fused_shards(): pl.pallas_call(functools.partial(fused_kernel, T), out_shape=jax.ShapeDty...  166 us

commit v1 on v0

v1 whole, which is shorter than its diff:
```python
import functools

import jax
import jax.numpy as jnp
from jax import lax
from jax.experimental import pallas as pl
from jax.experimental.pallas import tpu as pltpu
from jax.sharding import PartitionSpec as P

D = 4096
CAP = 160


epsilon = 1e-05
contract_width = (((1,), (1,)), ((), ()))
contract_hidden = (((0,), (1,)), ((), ()))
contract_slots = (((0,), (0,)), ((), ()))


def slot_matrix(ids_block, experts):
    flattened = ids_block.reshape(-1)
    onehot = (flattened[:, None] == jnp.arange(experts, dtype=jnp.int32)[None, :]).astype(jnp.int32)
    before = jnp.cumsum(onehot, axis=0) - onehot
    position = jnp.sum(before * onehot, axis=1)
    slot_index = flattened * CAP + position
    table = jnp.arange(experts * CAP, dtype=jnp.int32)
    return (slot_index[None, :] == table[:, None]).astype(jnp.bfloat16)


def shards(residual_stream, grad_output, norm_gain, expert_ids, gate_probs, w_gate, w_up, w_down):
    experts = lax.axis_size("expert")
    local_width = residual_stream.shape[1]
    tokens_here = residual_stream.shape[0]
    stream = residual_stream.astype(jnp.float32)
    squares = lax.psum(jnp.sum(stream * stream, axis=1), ("tensor", "kv"))
    inverse_rms = lax.rsqrt(squares / D + epsilon)[:, None]
    gains = norm_gain.astype(jnp.float32)
    normed = (stream * inverse_rms * gains).astype(jnp.bfloat16)
    table = slot_matrix(expert_ids, experts)
    repeated_x = jnp.repeat(normed, 2, axis=0)
    scaled = (
        jnp.repeat(grad_output.astype(jnp.float32), 2, axis=0) * gate_probs.reshape(-1, 1)
    ).astype(jnp.bfloat16)
    routed_x = jnp.dot(table, repeated_x, preferred_element_type=jnp.float32).astype(jnp.bfloat16)
    routed_grad = jnp.dot(table, scaled, preferred_element_type=jnp.float32).astype(jnp.bfloat16)
    routed_x = routed_x.reshape(experts, CAP, local_width)
    routed_grad = routed_grad.reshape(experts, CAP, local_width)
    gate_weight, up_weight, down_weight = (w_gate[0], w_up[0], w_down[0])
    pieces_x = lax.all_to_all(routed_x, "expert", split_axis=0, concat_axis=0, tiled=True)
    pieces_dy = lax.all_to_all(routed_grad, "expert", split_axis=0, concat_axis=0, tiled=True)
    full_x = lax.all_gather(pieces_x, ("tensor", "kv"), axis=2, tiled=True)
    full_dy = lax.all_gather(pieces_dy, ("tensor", "kv"), axis=2, tiled=True)
    leading = full_x.shape[0]
    items = full_x.shape[1]
    matrix_x = full_x.reshape(leading * items, D)
    matrix_dy = full_dy.reshape(leading * items, D)
    gate_value = lax.dot_general(
        matrix_x, gate_weight, contract_width, preferred_element_type=jnp.float32
    )
    up_value = lax.dot_general(
        matrix_x, up_weight, contract_width, preferred_element_type=jnp.float32
    )
    act_grad = lax.dot_general(
        matrix_dy, down_weight, contract_width, preferred_element_type=jnp.float32
    )
    sigmoid_gate = jax.nn.sigmoid(gate_value)
    activated = gate_value * sigmoid_gate
    gate_grad = (
        act_grad * up_value * sigmoid_gate * (1.0 + gate_value * (1.0 - sigmoid_gate))
    ).astype(jnp.bfloat16)
    up_grad = (act_grad * activated).astype(jnp.bfloat16)
    total = lax.dot_general(
        gate_weight, gate_grad, contract_hidden, preferred_element_type=jnp.float32
    )
    summed = lax.psum_scatter(
        total
        + lax.dot_general(up_weight, up_grad, contract_hidden, preferred_element_type=jnp.float32),
        ("tensor", "kv"),
        scatter_dimension=0,
        tiled=True,
    )
    returned = summed.T.astype(jnp.bfloat16).reshape(leading, items, local_width)
    combined = lax.all_to_all(returned, "expert", split_axis=0, concat_axis=0, tiled=True)
    gathered = lax.dot_general(
        table,
        combined.reshape(experts * CAP, local_width),
        contract_slots,
        preferred_element_type=jnp.float32,
    )
    token_grad = gathered.reshape(tokens_here, 2, local_width).sum(axis=1)
    scaled_grad = token_grad * gains
    projection = lax.psum(jnp.sum(scaled_grad * stream, axis=1), ("tensor", "kv"))[:, None]
    result = inverse_rms * scaled_grad - stream * inverse_rms**3 * projection / D
    return result.astype(jnp.bfloat16)


MESH = pl.DeviceIdType.MESH
TILE = 256
T = 4
BLOCKS = 2 * T
ORDER = [
    "1a0", "0f1", "1a1", "0g0", "0f0", "2a0", "C000", "D00", "1g0", "3a0", "C100", "C010", "0g1", "1g1", "0h0",
    "3a1", "D10", "0h1", "C001", "2g0", "D01", "2a1", "e1", "3g0", "2f0", "C101", "e0", "C030", "e2", "3f0",
    "3f1", "D30", "C020", "2f1", "e3", "3g1", "D20", "1x1", "C120", "1x0", "C130", "2h0", "2g1", "3h1", "C110",
    "C021", "3h0", "2h1", "D21", "1x2", "C031", "D31", "1x3", "C131", "C111", "C121", "C011", "D11",
]

EXTRA = [(1, 0, 1), (0, 1, 0), (0, 1, 1), (1, 1, 1)]
RETURN = [(d, s) for d in (1, 2, 3, 0) for s in (1, 0)]


def atoms_of(order):
    atoms, ahead = [], []
    for token in order:
        if token[0] == "C":
            atoms.append(dict(a=int(token[1]), i=int(token[2]), s=int(token[3]), ahead=ahead, middle=[]))
            ahead = []
        elif token[0] == "D":
            atoms[-1]["middle"], ahead = ahead, []
        else:
            ahead.append(token)
    return atoms, ahead


def pick(index, values):
    result = jnp.int32(values[0])
    for k, value in enumerate(values[1:], 1):
        if value != values[k - 1]:
            result = jnp.where(index >= k, value, result)
    return result


def fused_kernel(
    x_ref, dy_ref, gain_ref, ids_ref, prob_ref, wg_ref, wu_ref, wd_ref, out_ref,
    tok, acc, wab, wb, hid, routed, crecv, xrecv, yrecv, zrecv, gains, metas, sel, prob,
    ssq, own_sq, psend, precv, own_x, own_gain, own_meta,
    ag_send, ag_recv, line_send, line_recv, extra_send, extra_recv, rs_send, rs_recv,
    small_send, small_recv, wasem, wbsem, lsem,
):
    e = lax.axis_index("expert")
    z = lax.axis_index("tensor")
    y = lax.axis_index("kv")
    core = e + 1 - 2 * lax.rem(e, 2)
    across = lax.rem(e + 2, 4)
    partner = z + 1 - 2 * lax.rem(z, 2)
    tokens, width = out_ref.shape
    half = tokens // 2
    hidden = wg_ref.shape[0]
    tiles = hidden // TILE
    inputs = (x_ref, dy_ref)
    low = z < 2
    layer = [z, partner, jnp.where(low, 2, 1), jnp.where(low, 3, 0)]

    def z_of(d):
        return lax.rem(z + T - d, T)

    def y_of(s):
        return y if s == 0 else 1 - y

    def fb_of(d, s):
        return z_of(d) * 2 + y_of(s)

    def seen(i, s):
        return layer[i] * 2 + y_of(s)

    def b_of(u, c):
        base = core if c else e
        return lax.rem(base + 2 * u, 4)

    def remote(src, dst, send, recv, peer):
        return pltpu.make_async_remote_copy(
            src_ref=src, dst_ref=dst, send_sem=send, recv_sem=recv,
            device_id=peer, device_id_type=MESH,
        )

    def slot(a, i, s, u, c=0):
        return tok.at[a, seen(i, s), b_of(u, c)]

    def number(a, i, s, u, c):
        return (((a * T + i) * 2 + s) * 2 + u) * 2 + c

    across_peer, side_peer, core_peer = (across, z, y), (e, z, 1 - y), (core, z, y)

    def source(a, i, s, u):
        return inputs[a] if (i, s, u) == (0, 0, 0) else slot(a, i, s, u)

    def gather_copy(a, i, s, u, c=0):
        n = number(a, i, s, u, c)
        if c:
            src, there, peer = (s, u), slot(a, i, s, u), core_peer
        elif (u and not s) or (s and u and a == 0):
            src, peer = (s, 0), across_peer
            there = slot(a, i, s, 0)
        else:
            src, peer = (0, u), side_peer
            there = slot(a, i, 0, u)
        return remote(source(a, i, *src), there, ag_send.at[n], ag_recv.at[n], peer)

    def gather_wait(a, i, s, u, c=0):
        n = number(a, i, s, u, c)
        here = slot(a, i, s, u, c)
        remote(here, here, ag_send.at[n], ag_recv.at[n], core_peer).wait_recv()

    def extra_copy(k):
        a, s, u = EXTRA[k]
        here = slot(a, 0, s, u)
        return remote(here, here, extra_send.at[k], extra_recv.at[k], (e, partner, y))

    def extra_wait(k):
        a, s, u = EXTRA[k]
        here = slot(a, 1, s, u)
        remote(here, here, extra_send.at[k], extra_recv.at[k], (e, partner, y)).wait_recv()

    def own_line(a, way):
        return remote(
            inputs[a], tok.at[a, fb_of(0, 0), e], line_send.at[a, way], line_recv.at[a, z],
            (e, z + 2 * way - 1, y),
        )

    def pass_on(a, i):
        v = layer[i]
        here = slot(a, i, 0, 0)
        return remote(
            here, here, line_send.at[a, 1 + i], line_recv.at[a, v],
            (e, jnp.where(v < z, z + 1, z - 1), y),
        )

    def passes(i):
        return jnp.where(layer[i] < z, z < T - 1, z > 0)

    sent = []

    def send(*item):
        sent.append(item)
        gather_copy(*item).start()

    def full(i):
        return i != 1

    def event(token):
        if token[0] == "e":
            extra_copy(int(token[1])).start()
            return
        i, kind, k = int(token[0]), token[1], int(token[2])
        if kind == "a":
            pass_on(k, i).wait_recv()

            @pl.when(passes(i))
            def _():
                pass_on(k, i).start()

            if full(i):
                send(k, i, *((1, 0) if k == 0 else (0, 1)))
                send(k, i, *((0, 1) if k == 0 else (1, 0)))
            else:
                send(k, i, *((0, 1) if k == 0 else (1, 0)))
            send(k, i, 0, 0, 1)
            return
        if kind == "x":
            extra_wait(k)
            send(EXTRA[k][0], i, *EXTRA[k][1:], 1)
            return
        first = (1, 0) if k == 0 else (0, 1)
        s, u = {"f": first, "g": first[::-1], "h": (1, 1)}[kind]
        gather_wait(k, i, s, u)
        if kind == "f":
            send(k, i, 1, 1)
        send(k, i, s, u, 1)

    atoms, rest = atoms_of(ORDER)
    wide = [atom for atom in atoms if atom["a"] == 0]
    tall = [atom for atom in atoms if atom["a"] == 1]

    def fb_at(index, group):
        return select(index, [layer[atom["i"]] * 2 + y_of(atom["s"]) for atom in group])

    def select(index, values):
        result = values[0]
        for k, value in enumerate(values[1:], 1):
            result = jnp.where(index >= k, value, result)
        return result

    return_fb = [fb_of(*item) for item in RETURN]

    def columns_of(fb):
        return pl.ds(pl.multiple_of(fb * width, width), width)

    def wide_copies(index, place):
        columns = columns_of(place)
        at = lax.rem(index, 2)
        return [
            pltpu.make_async_copy(ref.at[:, columns], wab.at[at, k], wasem.at[at, k])
            for k, ref in enumerate((wg_ref, wu_ref))
        ]

    def tall_copy(index, place):
        at = lax.rem(index, 2)
        return pltpu.make_async_copy(wd_ref.at[:, columns_of(place)], wb.at[at], wbsem.at[at])

    local = [
        pltpu.make_async_copy(x_ref, tok.at[0, fb_of(0, 0), e], lsem.at[0]),
        pltpu.make_async_copy(dy_ref, tok.at[1, fb_of(0, 0), e], lsem.at[1]),
    ]
    peers = [(e, lax.rem(z + d, T), y_of(s)) for d in range(T) for s in (0, 1) if d or s]
    sources = [fb_of(d, s) for d in range(T) for s in (0, 1) if d or s]
    others = [(lax.rem(e + k, 4), z, y) for k in (1, 2, 3)]
    barrier = pltpu.get_barrier_semaphore()
    for peer in peers + others:
        pl.semaphore_signal(barrier, inc=1, device_id=peer, device_id_type=MESH)
    for copy in local:
        copy.start()
    pl.semaphore_wait(barrier, len(peers) + len(others))

    for a in (0, 1):
        for way in (0, 1):
            @pl.when(z < T - 1 if way else z > 0)
            def _():
                own_line(a, way).start()
    for item in ((0, 0, 1, 0), (1, 0, 0, 1), (0, 0, 0, 1), (1, 0, 1, 0), (0, 0, 0, 0, 1), (1, 0, 0, 0, 1)):
        send(*item)
    for copy in wide_copies(0, fb_at(0, wide)) + [tall_copy(0, fb_at(0, tall))]:
        copy.start()

    number_of = lax.broadcasted_iota(jnp.int32, (8, tokens), 0)
    named_by = jnp.where(number_of < 4, number_of, number_of - 4)
    first = jnp.broadcast_to(ids_ref[0:1, :], (8, tokens)) == named_by
    second = jnp.broadcast_to(ids_ref[1:2, :], (8, tokens)) == named_by
    named = jnp.where(first, 1.0, 0.0) + jnp.where(second, 1.0, 0.0)
    later = (
        lax.broadcasted_iota(jnp.int32, (tokens, tokens), 0)
        < lax.broadcasted_iota(jnp.int32, (tokens, tokens), 1)
    )
    before = jnp.dot(
        named.astype(jnp.bfloat16), jnp.where(later, 1.0, 0.0).astype(jnp.bfloat16),
        preferred_element_type=jnp.float32,
    )
    weight = jnp.where(first, jnp.broadcast_to(prob_ref[0:1, :], (8, tokens)), 0.0) + jnp.where(
        second, jnp.broadcast_to(prob_ref[1:2, :], (8, tokens)), 0.0
    )
    own_meta[...] = jnp.where(number_of < 4, jnp.where(named > 0.0, before, -1.0), weight)
    metas[e] = own_meta[...]
    own_gain[...] = jnp.broadcast_to(gain_ref[...].astype(jnp.float32)[None, :], own_gain.shape)
    gains[fb_of(0, 0)] = own_gain[...]

    small = []
    for k, peer in enumerate(others):
        copy = remote(own_meta, metas.at[e], small_send.at[k], small_recv.at[k], peer)
        copy.start()
        there = metas.at[lax.rem(e + 3 - k, 4)]
        small.append((copy, remote(there, there, small_send.at[k], small_recv.at[k], peer)))
    for k, peer in enumerate(peers):
        n = 3 + k
        copy = remote(own_gain, gains.at[fb_of(0, 0)], small_send.at[n], small_recv.at[n], peer)
        copy.start()
        there = gains.at[sources[k]]
        small.append((copy, remote(there, there, small_send.at[n], small_recv.at[n], peer)))

    own_sq[...] = jnp.zeros_like(own_sq)
    ssq[...] = jnp.zeros_like(ssq)

    def clear(n, carry):
        for k in range(3):
            acc[k, n] = jnp.zeros(acc.shape[2:], jnp.float32)
        return carry

    lax.fori_loop(0, tiles, clear, 0)
    for copy, arrival in small[:3]:
        arrival.wait_recv()
    for b in range(4):
        slots = metas[b, pl.ds(e, 1), :]
        probs = metas[b, pl.ds(4 + e, 1), :]
        index = lax.broadcasted_iota(jnp.int32, (CAP, slots.shape[1]), 0).astype(jnp.float32)
        chosen = jnp.where(index == slots, 1.0, 0.0)
        sel[b] = chosen.astype(jnp.bfloat16)
        prob[pl.ds(b * CAP, CAP), :] = jnp.sum(chosen * probs, axis=1, keepdims=True)
    for copy, arrival in small[3:]:
        arrival.wait_recv()
    for copy in local:
        copy.wait()

    def accumulate(k, source, weights):
        for n in range(tiles):
            acc[k, n] += lax.dot_general(
                source[...], weights[n * TILE : (n + 1) * TILE, :], contract_width,
                preferred_element_type=jnp.float32,
            )

    def gather_step(j, carry):
        for k, atom in enumerate(atoms):
            @pl.when(j == k)
            def _():
                for token in atom["ahead"]:
                    event(token)
                for u in (0, 1):
                    gather_wait(atom["a"], atom["i"], atom["s"], u, 1)

        kinds = [atom["a"] for atom in atoms]
        ranks = [sum(kinds[:k]) for k in range(len(atoms))]
        kind = pick(j, kinds)
        tall_rank = pick(j, ranks)
        wide_rank = j - tall_rank

        @pl.when(kind == 0)
        def _():
            following = jnp.where(
                wide_rank < BLOCKS - 1, fb_at(wide_rank + 1, wide), return_fb[0]
            )
            for copy in wide_copies(wide_rank + 1, following):
                copy.start()
            fb = fb_at(wide_rank, wide)
            gain_row = gains[fb, 0:1, :]
            mine = tok[0, fb, e].astype(jnp.float32)
            own_sq[...] += jnp.sum(mine * mine, axis=1, keepdims=True)
            for b in range(4):
                rows = pl.ds(b * CAP, CAP)
                picked = jnp.dot(sel[b], tok[0, fb, b], preferred_element_type=jnp.float32)
                ssq[rows, :] += jnp.sum(picked * picked, axis=1, keepdims=True)
                routed[0, rows, :] = (picked * gain_row).astype(jnp.bfloat16)
            for copy in wide_copies(wide_rank, fb):
                copy.wait()
            at = lax.rem(wide_rank, 2)
            accumulate(0, routed.at[0], wab.at[at, 0])
            for k, atom in enumerate(atoms):
                if atom["middle"]:
                    @pl.when(j == k)
                    def _():
                        for token in atom["middle"]:
                            event(token)
            accumulate(1, routed.at[0], wab.at[at, 1])

        @pl.when(kind == 1)
        def _():
            @pl.when(tall_rank < BLOCKS - 1)
            def _():
                tall_copy(tall_rank + 1, fb_at(tall_rank + 1, tall)).start()

            fb = fb_at(tall_rank, tall)
            for b in range(4):
                rows = pl.ds(b * CAP, CAP)
                picked = jnp.dot(sel[b], tok[1, fb, b], preferred_element_type=jnp.float32)
                routed[1, rows, :] = (picked * prob[rows, :]).astype(jnp.bfloat16)
            tall_copy(tall_rank, fb).wait()
            accumulate(2, routed.at[1], wb.at[lax.rem(tall_rank, 2)])

        return carry

    lax.fori_loop(0, len(atoms), gather_step, 0)
    for token in rest:
        event(token)
    reload = pltpu.make_async_copy(x_ref, own_x, lsem.at[2])
    reload.start()
    for item in sent:
        gather_copy(*item).wait_send()
    for a in (0, 1):
        for way in (0, 1):
            @pl.when(z < T - 1 if way else z > 0)
            def _():
                own_line(a, way).wait_send()
        for i in range(1, T):
            @pl.when(passes(i))
            def _():
                pass_on(a, i).wait_send()
    for k in range(len(EXTRA)):
        extra_copy(k).wait_send()
    for copy, arrival in small:
        copy.wait_send()

    inverse = lax.rsqrt(ssq[...] / D + epsilon)

    def activate(n, carry):
        columns = pl.ds(pl.multiple_of(n * TILE, TILE), TILE)
        gate_value = acc[0, n] * inverse
        up_value = acc[1, n] * inverse
        act_grad = acc[2, n]
        sigmoid_gate = jax.nn.sigmoid(gate_value)
        hid[0, :, columns] = (
            act_grad * up_value * sigmoid_gate * (1.0 + gate_value * (1.0 - sigmoid_gate))
        ).astype(jnp.bfloat16)
        hid[1, :, columns] = (act_grad * gate_value * sigmoid_gate).astype(jnp.bfloat16)
        return carry

    lax.fori_loop(0, tiles, activate, 0)

    upper, lower = pl.ds(0, half), pl.ds(half, half)

    def core_copy(i, u):
        return remote(
            tok.at[0, i, lax.rem(core + 2 * u, 4)], crecv.at[i, u],
            rs_send.at[i, u], rs_recv.at[i, u], core_peer,
        )

    def across_copy(i, h):
        rows = lower if h else upper
        return remote(
            tok.at[1, i, 0, rows], xrecv.at[i, rows], rs_send.at[i, 2 + h], rs_recv.at[i, 2 + h], across_peer
        )

    def side_copy(i, u, h):
        d = RETURN[i][0]
        rows = lower if h else upper
        n = 4 + (u if h else 2)
        return remote(
            tok.at[1, i, 0 if u else 1, rows], yrecv.at[d, u, rows], rs_send.at[i, n], rs_recv.at[i, n], side_peer
        )

    def line_copy(i):
        d = RETURN[i][0]
        return remote(
            tok.at[1, i, 2], zrecv.at[d - 1], rs_send.at[i, 7], rs_recv.at[i, 7], (e, z_of(d), y)
        )

    def total(rows, *parts):
        value = parts[0][rows].astype(jnp.float32)
        for part in parts[1:]:
            value = value + part[rows].astype(jnp.float32)
        return value

    everything = pl.ds(0, tokens)

    def first_stage(i):
        core_copy(i, 1).wait_recv()
        far = (tok.at[0, i, across], crecv.at[i, 1])
        if RETURN[i][1]:
            tok[1, i, 0] = total(everything, *far).astype(jnp.bfloat16)
            across_copy(i, 0).start()
            side_copy(i, 1, 1).start()
            core_copy(i, 0).wait_recv()
            tok[1, i, 1, lower] = total(lower, tok.at[0, i, e], crecv.at[i, 0]).astype(jnp.bfloat16)
            side_copy(i, 0, 1).start()
        else:
            tok[1, i, 0, upper] = total(upper, *far).astype(jnp.bfloat16)
            across_copy(i, 0).start()

    def second_stage(i):
        d, s = RETURN[i]
        if s:
            across_copy(i, 0).wait_recv()
            tok[1, i, 1, upper] = total(
                upper, tok.at[0, i, e], crecv.at[i, 0], xrecv.at[i]
            ).astype(jnp.bfloat16)
            side_copy(i, 0, 0).start()
        else:
            side_copy(i - 1, 1, 1).wait_recv()
            tok[1, i, 0, lower] = total(
                lower, tok.at[0, i, across], crecv.at[i, 1], yrecv.at[d, 1]
            ).astype(jnp.bfloat16)
            across_copy(i, 1).start()

    def third_stage(i):
        d = RETURN[i][0]
        core_copy(i, 0).wait_recv()
        across_copy(i, 0).wait_recv()
        side_copy(i - 1, 0, 1).wait_recv()
        side_copy(i - 1, 0, 0).wait_recv()
        across_copy(i, 1).wait_recv()
        value = total(everything, tok.at[0, i, e], crecv.at[i, 0], xrecv.at[i], yrecv.at[d, 0])
        if d:
            tok[1, i, 2] = value.astype(jnp.bfloat16)
            line_copy(i).start()
        return value

    halves = width // TILE
    stages = {}
    for i, (d, s) in enumerate(RETURN):
        base = halves * (i + 1)
        plan = [(1, first_stage), (4, second_stage)] if s else [(1, first_stage), (2, second_stage), (5, third_stage)]
        for when, stage in plan:
            stages.setdefault(base + when, []).append((stage, i))

    def produce(h, carry):
        for k in range(halves * BLOCKS):
            if k in stages:
                @pl.when(h == k)
                def _():
                    for stage, i in stages[k]:
                        stage(i)

        i, n = h // halves, lax.rem(h, halves)

        @pl.when(jnp.logical_and(n == 0, i < BLOCKS - 1))
        def _():
            for copy in wide_copies(i + 1, select(i + 1, return_fb)):
                copy.start()

        @pl.when(n == 0)
        def _():
            for copy in wide_copies(i, select(i, return_fb)):
                copy.wait()

        at = lax.rem(i, 2)
        columns = pl.ds(pl.multiple_of(n * TILE, TILE), TILE)
        rounded = (
            jnp.dot(hid[0], wab[at, 0, :, columns], preferred_element_type=jnp.float32)
            + jnp.dot(hid[1], wab[at, 1, :, columns], preferred_element_type=jnp.float32)
        ).astype(jnp.bfloat16)
        for b in range(4):
            tok[0, i, b, :, columns] = lax.dot_general(
                sel[b], rounded[b * CAP : (b + 1) * CAP], contract_slots,
                preferred_element_type=jnp.float32,
            ).astype(jnp.bfloat16)

        @pl.when(n == halves - 1)
        def _():
            core_copy(i, 1).start()
            core_copy(i, 0).start()

        return carry

    lax.fori_loop(0, halves * BLOCKS, produce, 0)
    value = None
    for key in sorted(stages):
        if key >= halves * BLOCKS:
            for stage, i in stages[key]:
                value = stage(i)
    reload.wait()
    for i in range(BLOCKS):
        if RETURN[i][1] == 0 and RETURN[i][0]:
            line_copy(i).wait_recv()
            value = value + zrecv[RETURN[i][0] - 1].astype(jnp.float32)

    gain_row = gains[fb_of(0, 0), 0:1, :]
    stream = own_x[...].astype(jnp.float32)
    scaled = value * gain_row
    share = jnp.sum(scaled * stream, axis=1, keepdims=True)
    psend[...] = jnp.broadcast_to(share, (tokens, 128)).T[0:8, :]
    final = []
    for k, peer in enumerate(peers):
        n = 3 + len(peers) + k
        copy = remote(psend, precv.at[k], small_send.at[n], small_recv.at[n], peer)
        copy.start()
        final.append(copy)
    inverse = lax.rsqrt(own_sq[...] / D + epsilon)
    row = psend[...]
    for k, copy in enumerate(final):
        copy.wait_recv()
        row = row + precv[k]
    projection = jnp.broadcast_to(row[0:1, :], (128, tokens)).T[:, 0:1]
    out_ref[...] = (
        inverse * scaled - stream * (inverse * inverse * inverse * projection / D)
    ).astype(out_ref.dtype)
    for copy in final:
        copy.wait_send()
    for i, (d, s) in enumerate(RETURN):
        core_copy(i, 0).wait_send()
        core_copy(i, 1).wait_send()
        across_copy(i, 0).wait_send()
        if s:
            side_copy(i, 1, 1).wait_send()
            side_copy(i, 0, 1).wait_send()
            side_copy(i, 0, 0).wait_send()
        else:
            across_copy(i, 1).wait_send()
            if d:
                line_copy(i).wait_send()


def fused_shards(residual_stream, grad_output, norm_gain, expert_ids, gate_probs, w_gate, w_up, w_down):
    experts = lax.axis_size("expert")
    tokens, width = residual_stream.shape
    hidden = w_gate.shape[1]
    bf16, f32 = jnp.bfloat16, jnp.float32
    rows = experts * CAP
    vmem = pl.BlockSpec(memory_space=pltpu.VMEM)
    hbm = pl.BlockSpec(memory_space=pl.ANY)
    dma = pltpu.SemaphoreType.DMA
    unit = (tokens, width)
    smalls = 3 + 2 * (BLOCKS - 1)
    return pl.pallas_call(
        fused_kernel,
        out_shape=jax.ShapeDtypeStruct(unit, bf16),
        in_specs=[hbm] * 2 + [vmem] * 3 + [hbm] * 3,
        out_specs=vmem,
        scratch_shapes=[
            pltpu.VMEM((2, BLOCKS, experts) + unit, bf16),
            pltpu.VMEM((3, hidden // TILE, rows, TILE), f32),
            pltpu.VMEM((2, 2, hidden, width), bf16),
            pltpu.VMEM((2, hidden, width), bf16),
            pltpu.VMEM((2, rows, hidden), bf16),
            pltpu.VMEM((2, rows, width), bf16),
            pltpu.VMEM((BLOCKS, 2) + unit, bf16),
            pltpu.VMEM((BLOCKS,) + unit, bf16),
            pltpu.VMEM((T, 2) + unit, bf16),
            pltpu.VMEM((T - 1,) + unit, bf16),
            pltpu.VMEM((BLOCKS, 8, width), f32),
            pltpu.VMEM((experts, 8, tokens), f32),
            pltpu.VMEM((experts, CAP, tokens), bf16),
            pltpu.VMEM((rows, 1), f32),
            pltpu.VMEM((rows, 1), f32),
            pltpu.VMEM((tokens, 1), f32),
            pltpu.VMEM((8, tokens), f32),
            pltpu.VMEM((BLOCKS - 1, 8, tokens), f32),
            pltpu.VMEM(unit, bf16),
            pltpu.VMEM((8, width), f32),
            pltpu.VMEM((8, tokens), f32),
            dma((16 * T,)),
            dma((16 * T,)),
            dma((2, T + 1)),
            dma((2, T)),
            dma((len(EXTRA),)),
            dma((len(EXTRA),)),
            dma((BLOCKS, 8)),
            dma((BLOCKS, 8)),
            dma((smalls,)),
            dma((smalls,)),
            dma((2, 2)),
            dma((2,)),
            dma((3,)),
        ],
        compiler_params=pltpu.CompilerParams(
            collective_id=0, has_side_effects=True, vmem_limit_bytes=66000000
        ),
        name="fused",
    )(
        residual_stream, grad_output, norm_gain, expert_ids.T, gate_probs.T,
        w_gate[0], w_up[0], w_down[0],
    )


def solution(mesh):
    placed = (
        P("expert", ("tensor", "kv")),
        P("expert", ("tensor", "kv")),
        P(("tensor", "kv")),
        P("expert", None),
        P("expert", None),
        P("expert", ("tensor", "kv"), None),
        P("expert", ("tensor", "kv"), None),
        P("expert", ("tensor", "kv"), None),
    )
    sizes = dict(mesh.shape)
    width = D // (sizes["tensor"] * sizes["kv"])
    body = fused_shards if sizes == {"expert": 4, "tensor": 4, "kv": 2} and width % 256 == 0 else shards
    return jax.shard_map(
        body, mesh=mesh, in_specs=placed, out_specs=P("expert", ("tensor", "kv")), check_vma=False
    )
```

time: 173 us -> 142 us (0.82)
  Pallas kernels: 166 us -> 141 us
  other arithmetic: 3.34 us -> 0 us
    pallas_call x1, Pallas kernels: 166 us -> 141 us  [fused_shards(): pl.pallas_call(fused_kernel, out_shape=jax.ShapeDtypeStruct(unit, bf16),...]
where the time goes in v1:
time: 142 us
  Pallas kernels  141 us (99%)
  local copies, waits for them, and re-layouts  1.67 us (1%)
    pallas_call x1, Pallas kernels, fused_shards(): pl.pallas_call(fused_kernel, out_shape=jax.ShapeDtypeStruct(unit, bf16),...  141 us

profile of v1, /device:TPU:0, one launch (start us, length us, event | category | flops | bytes accessed | tf_op | source)
XLA Modules:
  0.0 142.2 jit_solution(4792318554845373878)
XLA Ops:
  0.0 140.5 %fused.1 = bf16[256,512]{1,0:T(8,128)(2,1)} custom-call(bf16[256,512]{1,0:T(8,128)(2,1)} %x_ref.1, bf16[256,512]{1,0:T(8,128)(2,1)} %dy_ref.1, bf16[512]{0:T(512)(128)(2,1)} %gain_ref.1, s32[2,256]{1,0:T(2,128)} %bitcast.8, f32[2,256]{1,0:T(2,128)} %bitcast.9, bf16[1792,4096]{1,0:T(8,128)(2,1)} %bitcast.5, bf16[1792,4096]{1,0:T(8,128)(2,1)} %bitcast.6, ...), custom_call_target="tpu_custom_call" | custom-call | tf_op jit(solution)/shard_map/fused/pallas_call | solution.py:668
  140.5 1.7 %copy.10 = bf16[256,512]{1,0:T(8,128)(2,1)} copy(bf16[256,512]{1,0:T(8,128)(2,1)} %fused.1) | data formatting | bytes 524288

commit v2 on v1

--- a/solution.py
+++ b/solution.py
@@ -99,10 +99,10 @@
 T = 4
 BLOCKS = 2 * T
 ORDER = [
-    "1a0", "0f1", "1a1", "0g0", "0f0", "2a0", "C000", "D00", "1g0", "3a0", "C100", "C010", "0g1", "1g1", "0h0",
-    "3a1", "D10", "0h1", "C001", "2g0", "D01", "2a1", "e1", "3g0", "2f0", "C101", "e0", "C030", "e2", "3f0",
-    "3f1", "D30", "C020", "2f1", "e3", "3g1", "D20", "1x1", "C120", "1x0", "C130", "2h0", "2g1", "3h1", "C110",
-    "C021", "3h0", "2h1", "D21", "1x2", "C031", "D31", "1x3", "C131", "C111", "C121", "C011", "D11",
+    "0f0", "1a0", "0f1", "2a0", "1a1", "0g0", "2a1", "C000", "0h0", "D00", "C100", "0g1", "0h1", "3a0", "C001",
+    "D01", "1g0", "3a1", "2g0", "e2", "e0", "C010", "2f0", "2f1", "D10", "C020", "D20", "C120", "3g0", "1x2",
+    "C101", "3f0", "e1", "1g1", "C030", "3f1", "1x0", "2g1", "D30", "C130", "e3", "2h0", "C110", "1x1", "C021",
+    "2h1", "D21", "C011", "3h0", "D11", "C121", "3h1", "3g1", "1x3", "C031", "D31", "C111", "C131",
 ]
 
 EXTRA = [(1, 0, 1), (0, 1, 0), (0, 1, 1), (1, 1, 1)]
@@ -131,9 +131,9 @@
 
 
 def fused_kernel(
-    x_ref, dy_ref, gain_ref, ids_ref, prob_ref, wg_ref, wu_ref, wd_ref, out_ref,
+    x_ref, dy_ref, gain_hbm, ids_hbm, prob_hbm, wg_ref, wu_ref, wd_ref, out_ref,
     tok, acc, wab, wb, hid, routed, crecv, xrecv, yrecv, zrecv, gains, metas, sel, prob,
-    ssq, own_sq, psend, precv, own_x, own_gain, own_meta,
+    ssq, own_sq, psend, precv, ptotal, pothers, factor, own_x, own_gain, own_meta, gain_ref, ids_ref, prob_ref,
     ag_send, ag_recv, line_send, line_recv, extra_send, extra_recv, rs_send, rs_recv,
     small_send, small_recv, wasem, wbsem, lsem,
 ):
@@ -301,13 +301,18 @@
         pltpu.make_async_copy(x_ref, tok.at[0, fb_of(0, 0), e], lsem.at[0]),
         pltpu.make_async_copy(dy_ref, tok.at[1, fb_of(0, 0), e], lsem.at[1]),
     ]
+    tables = [
+        pltpu.make_async_copy(gain_hbm, gain_ref, lsem.at[3]),
+        pltpu.make_async_copy(ids_hbm, ids_ref, lsem.at[4]),
+        pltpu.make_async_copy(prob_hbm, prob_ref, lsem.at[5]),
+    ]
     peers = [(e, lax.rem(z + d, T), y_of(s)) for d in range(T) for s in (0, 1) if d or s]
     sources = [fb_of(d, s) for d in range(T) for s in (0, 1) if d or s]
     others = [(lax.rem(e + k, 4), z, y) for k in (1, 2, 3)]
     barrier = pltpu.get_barrier_semaphore()
     for peer in peers + others:
         pl.semaphore_signal(barrier, inc=1, device_id=peer, device_id_type=MESH)
-    for copy in local:
+    for copy in tables + local:
         copy.start()
     pl.semaphore_wait(barrier, len(peers) + len(others))
 
@@ -321,6 +326,8 @@
     for copy in wide_copies(0, fb_at(0, wide)) + [tall_copy(0, fb_at(0, tall))]:
         copy.start()
 
+    for copy in tables:
+        copy.wait()
     number_of = lax.broadcasted_iota(jnp.int32, (8, tokens), 0)
     named_by = jnp.where(number_of < 4, number_of, number_of - 4)
     first = jnp.broadcast_to(ids_ref[0:1, :], (8, tokens)) == named_by
@@ -385,14 +392,31 @@
                 preferred_element_type=jnp.float32,
             )
 
+    def dispatch(index, low, high, run, used):
+        if not any(k in used for k in range(low, high)):
+            return
+        if high - low == 1:
+            run(low)
+            return
+        middle = (low + high) // 2
+        for cond, first, last in ((index < middle, low, middle), (index >= middle, middle, high)):
+            if any(k in used for k in range(first, last)):
+                @pl.when(cond)
+                def _():
+                    dispatch(index, first, last, run, used)
+
     def gather_step(j, carry):
-        for k, atom in enumerate(atoms):
-            @pl.when(j == k)
-            def _():
-                for token in atom["ahead"]:
-                    event(token)
-                for u in (0, 1):
-                    gather_wait(atom["a"], atom["i"], atom["s"], u, 1)
+        def before_atom(k):
+            for token in atoms[k]["ahead"]:
+                event(token)
+            for u in (0, 1):
+                gather_wait(atoms[k]["a"], atoms[k]["i"], atoms[k]["s"], u, 1)
+
+        def amid_atom(k):
+            for token in atoms[k]["middle"]:
+                event(token)
+
+        dispatch(j, 0, len(atoms), before_atom, range(len(atoms)))
 
         kinds = [atom["a"] for atom in atoms]
         ranks = [sum(kinds[:k]) for k in range(len(atoms))]
@@ -420,12 +444,7 @@
                 copy.wait()
             at = lax.rem(wide_rank, 2)
             accumulate(0, routed.at[0], wab.at[at, 0])
-            for k, atom in enumerate(atoms):
-                if atom["middle"]:
-                    @pl.when(j == k)
-                    def _():
-                        for token in atom["middle"]:
-                            event(token)
+            dispatch(j, 0, len(atoms), amid_atom, [k for k, atom in enumerate(atoms) if atom["middle"]])
             accumulate(1, routed.at[0], wab.at[at, 1])
 
         @pl.when(kind == 1)
@@ -467,19 +486,68 @@
 
     inverse = lax.rsqrt(ssq[...] / D + epsilon)
 
-    def activate(n, carry):
+    def activate(n, start):
         columns = pl.ds(pl.multiple_of(n * TILE, TILE), TILE)
-        gate_value = acc[0, n] * inverse
-        up_value = acc[1, n] * inverse
-        act_grad = acc[2, n]
+        gate_sum, up_sum, act_grad = acc[0, n], acc[1, n], acc[2, n]
+        gate_value = gate_sum * inverse
+        up_value = up_sum * inverse
         sigmoid_gate = jax.nn.sigmoid(gate_value)
-        hid[0, :, columns] = (
+        gate_grad = (
             act_grad * up_value * sigmoid_gate * (1.0 + gate_value * (1.0 - sigmoid_gate))
         ).astype(jnp.bfloat16)
-        hid[1, :, columns] = (act_grad * gate_value * sigmoid_gate).astype(jnp.bfloat16)
+        up_grad = (act_grad * gate_value * sigmoid_gate).astype(jnp.bfloat16)
+        hid[0, :, columns] = gate_grad
+        hid[1, :, columns] = up_grad
+        term = gate_grad.astype(jnp.float32) * gate_sum + up_grad.astype(jnp.float32) * up_sum
+        acc[2, 0] = term if start else acc[2, 0] + term
+
+    def activate_more(n, carry):
+        activate(n, False)
         return carry
 
-    lax.fori_loop(0, tiles, activate, 0)
+    activate(0, True)
+    lax.fori_loop(1, tiles, activate_more, 0)
+
+    def share_copies():
+        return [
+            remote(psend, precv.at[k], small_send.at[10 + k], small_recv.at[10 + k], peer)
+            for k, peer in enumerate(peers)
+        ]
+
+    def total_copies():
+        return [
+            remote(ptotal, pothers.at[k], small_send.at[17 + k], small_recv.at[17 + k], peer)
+            for k, peer in enumerate(others)
+        ]
+
+    def share_projection():
+        pairs = jnp.sum(acc[2, 0], axis=1, keepdims=True)
+        for b in range(4):
+            of_block = sel[b].astype(jnp.float32) * pairs[b * CAP : (b + 1) * CAP]
+            psend[b : b + 1, :] = jnp.sum(of_block, axis=0, keepdims=True)
+        psend[4:8, :] = jnp.zeros((4, tokens), jnp.float32)
+        for copy in share_copies():
+            copy.start()
+
+    def total_projection():
+        for copy in share_copies():
+            copy.wait_recv()
+        row = psend[...]
+        for k in range(len(peers)):
+            row = row + precv[k]
+        ptotal[...] = row
+        for copy in total_copies():
+            copy.start()
+
+    def finish_projection():
+        for copy in total_copies():
+            copy.wait_recv()
+        row = ptotal[pl.ds(e, 1), :]
+        for k in range(len(others)):
+            row = row + pothers[k, pl.ds(e, 1), :]
+        projection = jnp.broadcast_to(row, (128, tokens)).T[:, 0:1]
+        inverse = lax.rsqrt(own_sq[...] / D + epsilon)
+        factor[...] = inverse * inverse * inverse * projection / D
 
     upper, lower = pl.ds(0, half), pl.ds(half, half)
 
@@ -568,12 +636,14 @@
             stages.setdefault(base + when, []).append((stage, i))
 
     def produce(h, carry):
-        for k in range(halves * BLOCKS):
-            if k in stages:
-                @pl.when(h == k)
-                def _():
-                    for stage, i in stages[k]:
-                        stage(i)
+        def run_stages(k):
+            for stage, i in stages.get(k, []):
+                stage(i)
+            for when, step in ((2, share_projection), (8, total_projection), (14, finish_projection)):
+                if k == when:
+                    step()
+
+        dispatch(h, 0, halves * BLOCKS, run_stages, [*stages, 2, 8, 14])
 
         i, n = h // halves, lax.rem(h, halves)
 
@@ -621,24 +691,9 @@
     gain_row = gains[fb_of(0, 0), 0:1, :]
     stream = own_x[...].astype(jnp.float32)
     scaled = value * gain_row
-    share = jnp.sum(scaled * stream, axis=1, keepdims=True)
-    psend[...] = jnp.broadcast_to(share, (tokens, 128)).T[0:8, :]
-    final = []
-    for k, peer in enumerate(peers):
-        n = 3 + len(peers) + k
-        copy = remote(psend, precv.at[k], small_send.at[n], small_recv.at[n], peer)
-        copy.start()
-        final.append(copy)
     inverse = lax.rsqrt(own_sq[...] / D + epsilon)
-    row = psend[...]
-    for k, copy in enumerate(final):
-        copy.wait_recv()
-        row = row + precv[k]
-    projection = jnp.broadcast_to(row[0:1, :], (128, tokens)).T[:, 0:1]
-    out_ref[...] = (
-        inverse * scaled - stream * (inverse * inverse * inverse * projection / D)
-    ).astype(out_ref.dtype)
-    for copy in final:
+    out_ref[...] = (inverse * scaled - stream * factor[...]).astype(out_ref.dtype)
+    for copy in share_copies() + total_copies():
         copy.wait_send()
     for i, (d, s) in enumerate(RETURN):
         core_copy(i, 0).wait_send()
@@ -664,11 +719,11 @@
     hbm = pl.BlockSpec(memory_space=pl.ANY)
     dma = pltpu.SemaphoreType.DMA
     unit = (tokens, width)
-    smalls = 3 + 2 * (BLOCKS - 1)
+    smalls = 3 + 2 * (BLOCKS - 1) + 3
     return pl.pallas_call(
         fused_kernel,
         out_shape=jax.ShapeDtypeStruct(unit, bf16),
-        in_specs=[hbm] * 2 + [vmem] * 3 + [hbm] * 3,
+        in_specs=[hbm] * 8,
         out_specs=vmem,
         scratch_shapes=[
             pltpu.VMEM((2, BLOCKS, experts) + unit, bf16),
@@ -689,9 +744,15 @@
             pltpu.VMEM((tokens, 1), f32),
             pltpu.VMEM((8, tokens), f32),
             pltpu.VMEM((BLOCKS - 1, 8, tokens), f32),
+            pltpu.VMEM((8, tokens), f32),
+            pltpu.VMEM((3, 8, tokens), f32),
+            pltpu.VMEM((tokens, 1), f32),
             pltpu.VMEM(unit, bf16),
             pltpu.VMEM((8, width), f32),
             pltpu.VMEM((8, tokens), f32),
+            pltpu.VMEM((width,), bf16),
+            pltpu.VMEM((2, tokens), jnp.int32),
+            pltpu.VMEM((2, tokens), f32),
             dma((16 * T,)),
             dma((16 * T,)),
             dma((2, T + 1)),
@@ -704,7 +765,7 @@
             dma((smalls,)),
             dma((2, 2)),
             dma((2,)),
-            dma((3,)),
+            dma((6,)),
         ],
         compiler_params=pltpu.CompilerParams(
             collective_id=0, has_side_effects=True, vmem_limit_bytes=66000000

time: 142 us -> 136 us (0.958)
  Pallas kernels: 141 us -> 134 us
    pallas_call x1, Pallas kernels: 141 us -> 134 us  [fused_shards(): pl.pallas_call(fused_kernel, out_shape=jax.ShapeDtypeStruct(unit, bf16),...]
where the time goes in v2:
time: 136 us
  Pallas kernels  134 us (99%)
  local copies, waits for them, and re-layouts  1.67 us (1%)
    pallas_call x1, Pallas kernels, fused_shards(): pl.pallas_call(fused_kernel, out_shape=jax.ShapeDtypeStruct(unit, bf16),...  134 us

profile of v2, /device:TPU:0, one launch (start us, length us, event | category | flops | bytes accessed | tf_op | source)
XLA Modules:
  0.0 136.1 jit_solution(12891906014787925676)
XLA Ops:
  0.0 134.4 %fused.1 = bf16[256,512]{1,0:T(8,128)(2,1)} custom-call(bf16[256,512]{1,0:T(8,128)(2,1)} %x_ref.1, bf16[256,512]{1,0:T(8,128)(2,1)} %dy_ref.1, bf16[512]{0:T(512)(128)(2,1)} %gain_hbm.1, s32[2,256]{1,0:T(2,128)} %bitcast.8, f32[2,256]{1,0:T(2,128)} %bitcast.9, bf16[1792,4096]{1,0:T(8,128)(2,1)} %bitcast.5, bf16[1792,4096]{1,0:T(8,128)(2,1)} %bitcast.6, ...), custom_call_target="tpu_custom_call" | custom-call | tf_op jit(solution)/shard_map/fused/pallas_call | solution.py:723
  134.4 1.7 %copy.10 = bf16[256,512]{1,0:T(8,128)(2,1)} copy(bf16[256,512]{1,0:T(8,128)(2,1)} %fused.1) | data formatting | bytes 524288

commit v3 on v2

--- a/solution.py
+++ b/solution.py
@@ -131,9 +131,9 @@
 
 
 def fused_kernel(
-    x_ref, dy_ref, gain_hbm, ids_hbm, prob_hbm, wg_ref, wu_ref, wd_ref, out_ref,
+    x_ref, dy_ref, gain_hbm, ids_hbm, prob_hbm, wg_ref, wu_ref, wd_ref, out_hbm,
     tok, acc, wab, wb, hid, routed, crecv, xrecv, yrecv, zrecv, gains, metas, sel, prob,
-    ssq, own_sq, psend, precv, ptotal, pothers, factor, own_x, own_gain, own_meta, gain_ref, ids_ref, prob_ref,
+    ssq, own_sq, own_inverse, psend, precv, ptotal, pothers, factor, own_x, own_gain, own_meta, gain_ref, ids_ref, prob_ref, out_ref,
     ag_send, ag_recv, line_send, line_recv, extra_send, extra_recv, rs_send, rs_recv,
     small_send, small_recv, wasem, wbsem, lsem,
 ):
@@ -385,6 +385,11 @@
     for copy in local:
         copy.wait()
 
+    def by_lane(value):
+        square = value * value
+        lanes = [square[:, k : k + 128] for k in range(0, width, 128)]
+        return sum(lanes[1:], lanes[0])
+
     def accumulate(k, source, weights):
         for n in range(tiles):
             acc[k, n] += lax.dot_general(
@@ -434,11 +439,11 @@
             fb = fb_at(wide_rank, wide)
             gain_row = gains[fb, 0:1, :]
             mine = tok[0, fb, e].astype(jnp.float32)
-            own_sq[...] += jnp.sum(mine * mine, axis=1, keepdims=True)
+            own_sq[...] += by_lane(mine)
             for b in range(4):
                 rows = pl.ds(b * CAP, CAP)
                 picked = jnp.dot(sel[b], tok[0, fb, b], preferred_element_type=jnp.float32)
-                ssq[rows, :] += jnp.sum(picked * picked, axis=1, keepdims=True)
+                ssq[rows, :] += by_lane(picked)
                 routed[0, rows, :] = (picked * gain_row).astype(jnp.bfloat16)
             for copy in wide_copies(wide_rank, fb):
                 copy.wait()
@@ -484,7 +489,7 @@
     for copy, arrival in small:
         copy.wait_send()
 
-    inverse = lax.rsqrt(ssq[...] / D + epsilon)
+    inverse = lax.rsqrt(jnp.sum(ssq[...], axis=1, keepdims=True) / D + epsilon)
 
     def activate(n, start):
         columns = pl.ds(pl.multiple_of(n * TILE, TILE), TILE)
@@ -546,104 +551,118 @@
         for k in range(len(others)):
             row = row + pothers[k, pl.ds(e, 1), :]
         projection = jnp.broadcast_to(row, (128, tokens)).T[:, 0:1]
-        inverse = lax.rsqrt(own_sq[...] / D + epsilon)
+        inverse = lax.rsqrt(jnp.sum(own_sq[...], axis=1, keepdims=True) / D + epsilon)
+        own_inverse[...] = inverse
         factor[...] = inverse * inverse * inverse * projection / D
 
-    upper, lower = pl.ds(0, half), pl.ds(half, half)
-
-    def core_copy(i, u):
+    upper, lower, everything = pl.ds(0, half), pl.ds(half, half), pl.ds(0, tokens)
+    halves = width // TILE
+
+    def place(m):
+        i, n = m // halves, m % halves
+        return i, *RETURN[i], pl.ds(n * TILE, TILE)
+
+    def core_copy(m, u):
+        i, n = m // halves, m % halves
+        columns = pl.ds(pl.multiple_of(n * TILE, TILE), TILE)
         return remote(
-            tok.at[0, i, lax.rem(core + 2 * u, 4)], crecv.at[i, u],
-            rs_send.at[i, u], rs_recv.at[i, u], core_peer,
+            tok.at[0, i, lax.rem(core + 2 * u, 4), :, columns], crecv.at[i, u, :, columns],
+            rs_send.at[m, u], rs_recv.at[m, u], core_peer,
         )
 
-    def across_copy(i, h):
+    def across_copy(m, h):
+        i, d, s, columns = place(m)
         rows = lower if h else upper
         return remote(
-            tok.at[1, i, 0, rows], xrecv.at[i, rows], rs_send.at[i, 2 + h], rs_recv.at[i, 2 + h], across_peer
+            tok.at[1, i, 0, rows, columns], xrecv.at[i, rows, columns],
+            rs_send.at[m, 2 + h], rs_recv.at[m, 2 + h], across_peer,
         )
 
-    def side_copy(i, u, h):
-        d = RETURN[i][0]
+    def side_copy(m, u, h):
+        i, d, s, columns = place(m)
         rows = lower if h else upper
         n = 4 + (u if h else 2)
         return remote(
-            tok.at[1, i, 0 if u else 1, rows], yrecv.at[d, u, rows], rs_send.at[i, n], rs_recv.at[i, n], side_peer
+            tok.at[1, i, 0 if u else 1, rows, columns], yrecv.at[d, u, rows, columns],
+            rs_send.at[m, n], rs_recv.at[m, n], side_peer,
         )
 
-    def line_copy(i):
-        d = RETURN[i][0]
+    def line_copy(m):
+        i, d, s, columns = place(m)
         return remote(
-            tok.at[1, i, 2], zrecv.at[d - 1], rs_send.at[i, 7], rs_recv.at[i, 7], (e, z_of(d), y)
+            tok.at[1, i, 2, :, columns], zrecv.at[d - 1, :, columns],
+            rs_send.at[m, 7], rs_recv.at[m, 7], (e, z_of(d), y),
         )
 
-    def total(rows, *parts):
-        value = parts[0][rows].astype(jnp.float32)
+    def total(rows, columns, *parts):
+        value = parts[0][rows, columns].astype(jnp.float32)
         for part in parts[1:]:
-            value = value + part[rows].astype(jnp.float32)
+            value = value + part[rows, columns].astype(jnp.float32)
         return value
 
-    everything = pl.ds(0, tokens)
-
-    def first_stage(i):
-        core_copy(i, 1).wait_recv()
+    def first_stage(m):
+        i, d, s, columns = place(m)
+        core_copy(m, 1).wait_recv()
         far = (tok.at[0, i, across], crecv.at[i, 1])
-        if RETURN[i][1]:
-            tok[1, i, 0] = total(everything, *far).astype(jnp.bfloat16)
-            across_copy(i, 0).start()
-            side_copy(i, 1, 1).start()
-            core_copy(i, 0).wait_recv()
-            tok[1, i, 1, lower] = total(lower, tok.at[0, i, e], crecv.at[i, 0]).astype(jnp.bfloat16)
-            side_copy(i, 0, 1).start()
+        if s:
+            tok[1, i, 0, :, columns] = total(everything, columns, *far).astype(jnp.bfloat16)
+            across_copy(m, 0).start()
+            side_copy(m, 1, 1).start()
+            core_copy(m, 0).wait_recv()
+            tok[1, i, 1, lower, columns] = total(
+                lower, columns, tok.at[0, i, e], crecv.at[i, 0]
+            ).astype(jnp.bfloat16)
+            side_copy(m, 0, 1).start()
         else:
-            tok[1, i, 0, upper] = total(upper, *far).astype(jnp.bfloat16)
-            across_copy(i, 0).start()
-
-    def second_stage(i):
-        d, s = RETURN[i]
+            tok[1, i, 0, upper, columns] = total(upper, columns, *far).astype(jnp.bfloat16)
+            across_copy(m, 0).start()
+
+    def second_stage(m):
+        i, d, s, columns = place(m)
         if s:
-            across_copy(i, 0).wait_recv()
-            tok[1, i, 1, upper] = total(
-                upper, tok.at[0, i, e], crecv.at[i, 0], xrecv.at[i]
+            across_copy(m, 0).wait_recv()
+            tok[1, i, 1, upper, columns] = total(
+                upper, columns, tok.at[0, i, e], crecv.at[i, 0], xrecv.at[i]
             ).astype(jnp.bfloat16)
-            side_copy(i, 0, 0).start()
+            side_copy(m, 0, 0).start()
         else:
-            side_copy(i - 1, 1, 1).wait_recv()
-            tok[1, i, 0, lower] = total(
-                lower, tok.at[0, i, across], crecv.at[i, 1], yrecv.at[d, 1]
+            side_copy(m - halves, 1, 1).wait_recv()
+            tok[1, i, 0, lower, columns] = total(
+                lower, columns, tok.at[0, i, across], crecv.at[i, 1], yrecv.at[d, 1]
             ).astype(jnp.bfloat16)
-            across_copy(i, 1).start()
-
-    def third_stage(i):
-        d = RETURN[i][0]
-        core_copy(i, 0).wait_recv()
-        across_copy(i, 0).wait_recv()
-        side_copy(i - 1, 0, 1).wait_recv()
-        side_copy(i - 1, 0, 0).wait_recv()
-        across_copy(i, 1).wait_recv()
-        value = total(everything, tok.at[0, i, e], crecv.at[i, 0], xrecv.at[i], yrecv.at[d, 0])
+            across_copy(m, 1).start()
+
+    def third_stage(m):
+        i, d, s, columns = place(m)
+        core_copy(m, 0).wait_recv()
+        across_copy(m, 0).wait_recv()
+        side_copy(m - halves, 0, 1).wait_recv()
+        side_copy(m - halves, 0, 0).wait_recv()
+        across_copy(m, 1).wait_recv()
+        value = total(everything, columns, tok.at[0, i, e], crecv.at[i, 0], xrecv.at[i], yrecv.at[d, 0])
         if d:
-            tok[1, i, 2] = value.astype(jnp.bfloat16)
-            line_copy(i).start()
-        return value
-
-    halves = width // TILE
+            tok[1, i, 2, :, columns] = value.astype(jnp.bfloat16)
+            line_copy(m).start()
+        else:
+            acc[0, m % halves, everything, :] = value
+
     stages = {}
-    for i, (d, s) in enumerate(RETURN):
-        base = halves * (i + 1)
-        plan = [(1, first_stage), (4, second_stage)] if s else [(1, first_stage), (2, second_stage), (5, third_stage)]
+    for m in range(halves * BLOCKS):
+        plan = [(1, first_stage), (4, second_stage)] if place(m)[2] else (
+            [(1, first_stage), (2, second_stage), (5, third_stage)]
+        )
         for when, stage in plan:
-            stages.setdefault(base + when, []).append((stage, i))
+            stages.setdefault(m + 1 + when, []).append((stage, m))
 
     def produce(h, carry):
         def run_stages(k):
             for stage, i in stages.get(k, []):
                 stage(i)
-            for when, step in ((2, share_projection), (8, total_projection), (14, finish_projection)):
+            for when, step in ((6, share_projection), (10, total_projection), (15, finish_projection)):
                 if k == when:
                     step()
 
-        dispatch(h, 0, halves * BLOCKS, run_stages, [*stages, 2, 8, 14])
+        dispatch(h, 0, halves * BLOCKS, run_stages, [*stages, 6, 10, 15])
 
         i, n = h // halves, lax.rem(h, halves)
 
@@ -669,44 +688,44 @@
                 preferred_element_type=jnp.float32,
             ).astype(jnp.bfloat16)
 
-        @pl.when(n == halves - 1)
-        def _():
-            core_copy(i, 1).start()
-            core_copy(i, 0).start()
-
+        core_copy(h, 1).start()
+        core_copy(h, 0).start()
         return carry
 
     lax.fori_loop(0, halves * BLOCKS, produce, 0)
-    value = None
     for key in sorted(stages):
         if key >= halves * BLOCKS:
-            for stage, i in stages[key]:
-                value = stage(i)
+            for stage, m in stages[key]:
+                stage(m)
     reload.wait()
-    for i in range(BLOCKS):
-        if RETURN[i][1] == 0 and RETURN[i][0]:
-            line_copy(i).wait_recv()
-            value = value + zrecv[RETURN[i][0] - 1].astype(jnp.float32)
-
-    gain_row = gains[fb_of(0, 0), 0:1, :]
-    stream = own_x[...].astype(jnp.float32)
-    scaled = value * gain_row
-    inverse = lax.rsqrt(own_sq[...] / D + epsilon)
-    out_ref[...] = (inverse * scaled - stream * factor[...]).astype(out_ref.dtype)
+    for n in range(halves):
+        columns = pl.ds(n * TILE, TILE)
+        value = acc[0, n, everything, :]
+        for i, (d, s) in enumerate(RETURN):
+            if d and not s:
+                line_copy(halves * i + n).wait_recv()
+                value = value + zrecv[d - 1, :, columns].astype(jnp.float32)
+        scaled = value * gains[fb_of(0, 0), 0:1, columns]
+        stream = own_x[:, columns].astype(jnp.float32)
+        out_ref[:, columns] = (own_inverse[...] * scaled - stream * factor[...]).astype(out_ref.dtype)
+    written = pltpu.make_async_copy(out_ref, out_hbm, lsem.at[2])
+    written.start()
     for copy in share_copies() + total_copies():
         copy.wait_send()
-    for i, (d, s) in enumerate(RETURN):
-        core_copy(i, 0).wait_send()
-        core_copy(i, 1).wait_send()
-        across_copy(i, 0).wait_send()
+    for m in range(halves * BLOCKS):
+        i, d, s, columns = place(m)
+        core_copy(m, 0).wait_send()
+        core_copy(m, 1).wait_send()
+        across_copy(m, 0).wait_send()
         if s:
-            side_copy(i, 1, 1).wait_send()
-            side_copy(i, 0, 1).wait_send()
-            side_copy(i, 0, 0).wait_send()
+            side_copy(m, 1, 1).wait_send()
+            side_copy(m, 0, 1).wait_send()
+            side_copy(m, 0, 0).wait_send()
         else:
-            across_copy(i, 1).wait_send()
+            across_copy(m, 1).wait_send()
             if d:
-                line_copy(i).wait_send()
+                line_copy(m).wait_send()
+    written.wait()
 
 
 def fused_shards(residual_stream, grad_output, norm_gain, expert_ids, gate_probs, w_gate, w_up, w_down):
@@ -715,7 +734,6 @@
     hidden = w_gate.shape[1]
     bf16, f32 = jnp.bfloat16, jnp.float32
     rows = experts * CAP
-    vmem = pl.BlockSpec(memory_space=pltpu.VMEM)
     hbm = pl.BlockSpec(memory_space=pl.ANY)
     dma = pltpu.SemaphoreType.DMA
     unit = (tokens, width)
@@ -724,7 +742,7 @@
         fused_kernel,
         out_shape=jax.ShapeDtypeStruct(unit, bf16),
         in_specs=[hbm] * 8,
-        out_specs=vmem,
+        out_specs=hbm,
         scratch_shapes=[
             pltpu.VMEM((2, BLOCKS, experts) + unit, bf16),
             pltpu.VMEM((3, hidden // TILE, rows, TILE), f32),
@@ -740,7 +758,8 @@
             pltpu.VMEM((experts, 8, tokens), f32),
             pltpu.VMEM((experts, CAP, tokens), bf16),
             pltpu.VMEM((rows, 1), f32),
-            pltpu.VMEM((rows, 1), f32),
+            pltpu.VMEM((rows, 128), f32),
+            pltpu.VMEM((tokens, 128), f32),
             pltpu.VMEM((tokens, 1), f32),
             pltpu.VMEM((8, tokens), f32),
             pltpu.VMEM((BLOCKS - 1, 8, tokens), f32),
@@ -753,14 +772,15 @@
             pltpu.VMEM((width,), bf16),
             pltpu.VMEM((2, tokens), jnp.int32),
             pltpu.VMEM((2, tokens), f32),
+            pltpu.VMEM(unit, bf16),
             dma((16 * T,)),
             dma((16 * T,)),
             dma((2, T + 1)),
             dma((2, T)),
             dma((len(EXTRA),)),
             dma((len(EXTRA),)),
-            dma((BLOCKS, 8)),
-            dma((BLOCKS, 8)),
+            dma((width // TILE * BLOCKS, 8)),
+            dma((width // TILE * BLOCKS, 8)),
             dma((smalls,)),
             dma((smalls,)),
             dma((2, 2)),

time: 136 us -> 135 us (level)
  no operation moved by 1% of the time
where the time goes in v3:
time: 135 us
  Pallas kernels  133 us (99%)
  local copies, waits for them, and re-layouts  1.67 us (1%)
    pallas_call x1, Pallas kernels, fused_shards(): pl.pallas_call(fused_kernel, out_shape=jax.ShapeDtypeStruct(unit, bf16),...  133 us

profile of v3, /device:TPU:0, one launch (start us, length us, event | category | flops | bytes accessed | tf_op | source)
XLA Modules:
  0.0 134.7 jit_solution(8051737075750590991)
XLA Ops:
  0.0 133.0 %fused.1 = bf16[256,512]{1,0:T(8,128)(2,1)} custom-call(bf16[256,512]{1,0:T(8,128)(2,1)} %x_ref.1, bf16[256,512]{1,0:T(8,128)(2,1)} %dy_ref.1, bf16[512]{0:T(512)(128)(2,1)} %gain_hbm.1, s32[2,256]{1,0:T(2,128)} %bitcast.8, f32[2,256]{1,0:T(2,128)} %bitcast.9, bf16[1792,4096]{1,0:T(8,128)(2,1)} %bitcast.5, bf16[1792,4096]{1,0:T(8,128)(2,1)} %bitcast.6, ...), custom_call_target="tpu_custom_call" | custom-call | tf_op jit(solution)/shard_map/fused/pallas_call | solution.py:741
  133.1 1.7 %copy.10 = bf16[256,512]{1,0:T(8,128)(2,1)} copy(bf16[256,512]{1,0:T(8,128)(2,1)} %fused.1) | data formatting | bytes 524288

commit v4 on v3

--- a/solution.py
+++ b/solution.py
@@ -654,15 +654,17 @@
         for when, stage in plan:
             stages.setdefault(m + 1 + when, []).append((stage, m))
 
+    projection_steps = {2: share_projection, 9: total_projection, 15: finish_projection}
+
+    def run_stages(k):
+        for stage, m in stages.get(k, []):
+            stage(m)
+        if k in projection_steps:
+            projection_steps[k]()
+
     def produce(h, carry):
-        def run_stages(k):
-            for stage, i in stages.get(k, []):
-                stage(i)
-            for when, step in ((6, share_projection), (10, total_projection), (15, finish_projection)):
-                if k == when:
-                    step()
-
-        dispatch(h, 0, halves * BLOCKS, run_stages, [*stages, 6, 10, 15])
+
+        dispatch(h, 0, halves * BLOCKS, run_stages, [*stages, *projection_steps])
 
         i, n = h // halves, lax.rem(h, halves)
 
@@ -693,10 +695,9 @@
         return carry
 
     lax.fori_loop(0, halves * BLOCKS, produce, 0)
-    for key in sorted(stages):
+    for key in sorted({*stages, *projection_steps}):
         if key >= halves * BLOCKS:
-            for stage, m in stages[key]:
-                stage(m)
+            run_stages(key)
     reload.wait()
     for n in range(halves):
         columns = pl.ds(n * TILE, TILE)

time: 135 us -> 135 us (level)
  no operation moved by 1% of the time
where the time goes in v4:
time: 135 us
  Pallas kernels  133 us (99%)
  local copies, waits for them, and re-layouts  1.67 us (1%)
    pallas_call x1, Pallas kernels, fused_shards(): pl.pallas_call(fused_kernel, out_shape=jax.ShapeDtypeStruct(unit, bf16),...  133 us

profile of v4, /device:TPU:0, one launch (start us, length us, event | category | flops | bytes accessed | tf_op | source)
XLA Modules:
  0.0 134.7 jit_solution(7778967151717224722)
XLA Ops:
  0.0 133.1 %fused.1 = bf16[256,512]{1,0:T(8,128)(2,1)} custom-call(bf16[256,512]{1,0:T(8,128)(2,1)} %x_ref.1, bf16[256,512]{1,0:T(8,128)(2,1)} %dy_ref.1, bf16[512]{0:T(512)(128)(2,1)} %gain_hbm.1, s32[2,256]{1,0:T(2,128)} %bitcast.8, f32[2,256]{1,0:T(2,128)} %bitcast.9, bf16[1792,4096]{1,0:T(8,128)(2,1)} %bitcast.5, bf16[1792,4096]{1,0:T(8,128)(2,1)} %bitcast.6, ...), custom_call_target="tpu_custom_call" | custom-call | tf_op jit(solution)/shard_map/fused/pallas_call | solution.py:742
  133.1 1.7 %copy.10 = bf16[256,512]{1,0:T(8,128)(2,1)} copy(bf16[256,512]{1,0:T(8,128)(2,1)} %fused.1) | data formatting | bytes 524288

commit v5 on v4

--- a/solution.py
+++ b/solution.py
@@ -316,13 +316,15 @@
         copy.start()
     pl.semaphore_wait(barrier, len(peers) + len(others))
 
+    for item in ((0, 0, 1, 0), (1, 0, 0, 1), (0, 0, 0, 1), (1, 0, 1, 0)):
+        send(*item)
     for a in (0, 1):
         for way in (0, 1):
             @pl.when(z < T - 1 if way else z > 0)
             def _():
                 own_line(a, way).start()
-    for item in ((0, 0, 1, 0), (1, 0, 0, 1), (0, 0, 0, 1), (1, 0, 1, 0), (0, 0, 0, 0, 1), (1, 0, 0, 0, 1)):
-        send(*item)
+    for a in (0, 1):
+        send(a, 0, 0, 0, 1)
     for copy in wide_copies(0, fb_at(0, wide)) + [tall_copy(0, fb_at(0, tall))]:
         copy.start()
 

time: 135 us -> 135 us (level)
  no operation moved by 1% of the time
where the time goes in v5:
time: 135 us
  Pallas kernels  133 us (99%)
  local copies, waits for them, and re-layouts  1.67 us (1%)
    pallas_call x1, Pallas kernels, fused_shards(): pl.pallas_call(fused_kernel, out_shape=jax.ShapeDtypeStruct(unit, bf16),...  133 us

profile of v5, /device:TPU:0, one launch (start us, length us, event | category | flops | bytes accessed | tf_op | source)
XLA Modules:
  0.0 134.8 jit_solution(1939140617110826631)
XLA Ops:
  0.0 133.1 %fused.1 = bf16[256,512]{1,0:T(8,128)(2,1)} custom-call(bf16[256,512]{1,0:T(8,128)(2,1)} %x_ref.1, bf16[256,512]{1,0:T(8,128)(2,1)} %dy_ref.1, bf16[512]{0:T(512)(128)(2,1)} %gain_hbm.1, s32[2,256]{1,0:T(2,128)} %bitcast.8, f32[2,256]{1,0:T(2,128)} %bitcast.9, bf16[1792,4096]{1,0:T(8,128)(2,1)} %bitcast.5, bf16[1792,4096]{1,0:T(8,128)(2,1)} %bitcast.6, ...), custom_call_target="tpu_custom_call" | custom-call | tf_op jit(solution)/shard_map/fused/pallas_call | solution.py:744
  133.1 1.7 %copy.10 = bf16[256,512]{1,0:T(8,128)(2,1)} copy(bf16[256,512]{1,0:T(8,128)(2,1)} %fused.1) | data formatting | bytes 524288
